TPU v7x, 256 devices: a whole 4x4x8 slice. The times are simulated.
256 devices in a mesh: sub: 32 (over x, z_hi, core), coarse: 8 (over z_lo, y).
Axes of the slice: x: 4, y: 4, z: 8 (z_hi: 4, z_lo: 2; z = z_hi * 2 + z_lo), core: 2. Of those that a mesh axis runs over, the one named last changes fastest.
Arguments:
- residual_parts: bfloat16 [32, 8, 4, 256, 512], P('sub', 'coarse'), may hold values from -6 to 6
- face_slot: int32 [32, 8, 4], P('sub', 'coarse'), may hold values from 0 to 3, each once within a row
- face_order: int32 [32, 8, 4, 512], P('sub', 'coarse'), may hold values from 0 to 511, each once within a row
- face_scale: float32 [32, 8, 4], P('sub', 'coarse'), may hold values from 0 to 1, as said below
- vertex_unknowns: int32 [32, 8, 256], P('sub', 'coarse'), may hold values from 0 to 2047, all different within a row
- front_inverse: bfloat16 [32, 8, 2048, 2048], P('sub', 'coarse')
- coarse_basis: bfloat16 [32, 8, 2048, 256], P('sub', 'coarse'), may hold values from -0.125 to 0.125
- coarse_inverse: bfloat16 [32, 2048, 2048], P('sub', None, 'coarse'), as said below
- thermal_handoff: bfloat16 [32, 2048, 128], P('sub'), may hold values from -0.125 to 0.125
- chain_transfer: float32 [32, 128, 128], P('sub')
- coupling_in: bfloat16 [32, 128, 2048], P('sub', None, 'coarse'), may hold values from -0.5 to 0.5
Outputs:
- correction: bfloat16 [32, 8, 4, 256, 512], P('sub', 'coarse')
Inputs may be any that keep to these rules, and one draw needn't show every extreme that they name: `face_slot`: each row is a permutation of 0 to 3. `face_order`: each row is a permutation of 0 to 511. `vertex_unknowns`: the 256 entries of each subdomain are distinct. `face_scale`: the two weights of a shared face sum to one; a face on the outer boundary has weight one. `coarse_inverse`: each line's matrix is symmetric.
All inputs are finite; a program needn't handle non-finite values.
Results may differ from a plain program's by a relative error of at most 0.0059.
Values may be sent and summed in bfloat16 or wider, within the bound.
No kernel may reach another device: no remote copies, remote signals or barrier semaphores. Data moves between devices by JAX's collectives and lax.ppermute only.
A program may use at most 128 MiB of HBM per device.

v0:
```python
import jax
import jax.numpy as jnp
from jax import lax
from jax.sharding import PartitionSpec as P

HIGHEST = lax.Precision.HIGHEST


def with_halo(block, sides, width):
    for axis, dim in sides:
        count = lax.axis_size(axis)
        forward = [(i, i + 1) for i in range(count - 1)]
        backward = [(target, source) for source, target in forward]
        low = lax.ppermute(
            lax.slice_in_dim(block, block.shape[dim] - width, None, axis=dim), axis, forward
        )
        high = lax.ppermute(lax.slice_in_dim(block, 0, width, axis=dim), axis, backward)
        block = jnp.concatenate([low, block, high], axis=dim)
    return block


def carried_in(array, axis, combine, identity):
    peers, mine = (lax.axis_size(axis), lax.axis_index(axis))
    everything = jax.tree.map(lambda part: lax.all_gather(part, axis), array)
    start = jax.tree.map(
        lambda part, zero: jnp.broadcast_to(jnp.asarray(zero, part.dtype), part.shape),
        array,
        identity,
    )

    def step(k, before):
        reached = k < mine
        new = combine(before, jax.tree.map(lambda part: part[k], everything))
        return jax.tree.map(lambda a, b: jnp.where(reached, a, b), new, before)

    return lax.fori_loop(0, peers, step, start)


def build_tables(face_slot, face_order, table_type):
    face_count, block_size = face_order.shape
    slot_table = (
        face_slot[:, None] == lax.broadcasted_iota(jnp.int32, (face_count, face_count), 1)
    ).astype(table_type)
    order_table = (
        face_order[:, :, None]
        == lax.broadcasted_iota(jnp.int32, (face_count, block_size, block_size), 2)
    ).astype(table_type)
    return (slot_table, order_table)


def to_canonical(values, tables):
    slot_table, order_table = tables
    ordered = jnp.einsum(
        "snk,sjk->snj", values, order_table, preferred_element_type=jnp.float32, precision=HIGHEST
    ).astype(values.dtype)
    return jnp.einsum(
        "ds,snj->dnj", slot_table, ordered, preferred_element_type=jnp.float32, precision=HIGHEST
    ).astype(values.dtype)


def from_canonical(values, tables):
    slot_table, order_table = tables
    by_face = jnp.einsum(
        "ds,dnj->snj", slot_table, values, preferred_element_type=jnp.float32, precision=HIGHEST
    ).astype(values.dtype)
    return jnp.einsum(
        "snj,sjk->snk", by_face, order_table, preferred_element_type=jnp.float32, precision=HIGHEST
    ).astype(values.dtype)


def trade_faces(face_values):
    along_sub = with_halo(face_values[0:2], (("sub", 0),), 1)
    along_coarse = with_halo(face_values[2:4], (("coarse", 0),), 1)
    return jnp.stack([along_sub[0], along_sub[3], along_coarse[0], along_coarse[3]], 0)


def per_device(
    residual_parts,
    face_slot,
    face_order,
    face_scale,
    vertex_unknowns,
    front_inverse,
    coarse_basis,
    coarse_inverse,
    thermal_handoff,
    chain_transfer,
    coupling_in,
):
    own_parts = residual_parts[0, 0]
    own_slot = face_slot[0, 0]
    own_order = face_order[0, 0]
    own_scale = face_scale[0, 0][:, None, None]
    face_count, sample_count, block_size = own_parts.shape
    reduced_precision_tables = build_tables(own_slot, own_order, jnp.bfloat16)
    canon = to_canonical(own_parts, reduced_precision_tables)
    beside = trade_faces(canon)
    averaged = (own_scale * (canon.astype(jnp.float32) + beside.astype(jnp.float32))).astype(
        jnp.bfloat16
    )
    local_residual = from_canonical(averaged, reduced_precision_tables)
    own_primal = vertex_unknowns[0, 0]
    positions = lax.broadcasted_iota(jnp.int32, (own_primal.shape[0], face_count * block_size), 1)
    hits = jnp.sum((own_primal[:, None] == positions).astype(jnp.int32), axis=0)
    dual_mask = (1 - hits).astype(jnp.bfloat16).reshape(face_count, 1, block_size)
    inverse_blocks = front_inverse[0, 0].reshape(face_count, block_size, face_count, block_size)
    dual_part = (
        jnp.einsum(
            "gnj,gjfk->fnk",
            local_residual * dual_mask,
            inverse_blocks,
            preferred_element_type=jnp.float32,
        )
        * dual_mask
    )
    basis_blocks = coarse_basis[0, 0].reshape(face_count, block_size, -1)
    coarse_residual = jnp.einsum(
        "gnj,gjc->nc", local_residual, basis_blocks, preferred_element_type=jnp.float32
    ).astype(jnp.bfloat16)
    primal_count = coarse_residual.shape[1]
    line_block = coarse_inverse[0]
    line_outflow = thermal_handoff[0]
    channel_count = line_outflow.shape[1]
    line_base = lax.dot_general(
        line_block,
        lax.all_gather(coarse_residual, "coarse", axis=1, tiled=True),
        (((0,), (1,)), ((), ())),
        preferred_element_type=jnp.float32,
    )
    own_rows = lax.dynamic_slice_in_dim(
        line_outflow, lax.axis_index("coarse") * primal_count, primal_count, 0
    )
    inflow = lax.psum(
        jnp.dot(coarse_residual, own_rows, preferred_element_type=jnp.float32), "coarse"
    )
    transfer = chain_transfer[0]

    def compose(earlier, later):
        joined_map = jnp.dot(earlier[0], later[0], precision=HIGHEST)
        joined_state = jnp.dot(earlier[1], later[0], precision=HIGHEST) + later[1]
        return (joined_map, joined_state)

    identity = (jnp.eye(channel_count, dtype=jnp.float32), jnp.zeros_like(inflow))
    upstream_map, carried = carried_in((transfer, inflow), "sub", compose, identity)
    carried_term = lax.dot_general(
        coupling_in[0].astype(jnp.float32), carried, (((0,), (1,)), ((), ())), precision=HIGHEST
    )
    global_coarse_answer = (line_base + carried_term).astype(jnp.bfloat16)
    subregion_iterate = dual_part + jnp.einsum(
        "cn,gjc->gnj", global_coarse_answer, basis_blocks, preferred_element_type=jnp.float32
    )
    exact_tables = build_tables(own_slot, own_order, jnp.float32)
    weighted = (own_scale * to_canonical(subregion_iterate, exact_tables)).astype(jnp.bfloat16)
    beside_again = trade_faces(weighted)
    summed = (weighted.astype(jnp.float32) + beside_again.astype(jnp.float32)).astype(jnp.bfloat16)
    return from_canonical(summed, reduced_precision_tables)[None, None]


def solution(mesh):
    placed = (
        P("sub", "coarse", None, None, None),
        P("sub", "coarse", None),
        P("sub", "coarse", None, None),
        P("sub", "coarse", None),
        P("sub", "coarse", None),
        P("sub", "coarse", None, None),
        P("sub", "coarse", None, None),
        P("sub", None, "coarse"),
        P("sub", None, None),
        P("sub", None, None),
        P("sub", None, "coarse"),
    )
    return jax.shard_map(
        per_device,
        mesh=mesh,
        in_specs=placed,
        out_specs=P("sub", "coarse", None, None, None),
        check_vma=False,
    )
```

profile of v0, /device:TPU:26, one launch (start us, length us, event | category | flops | bytes accessed | tf_op | source)
XLA Modules:
  0.0 419.8 jit_solution(5209459540740825076)
XLA Ops:
  6.5 2.4 fusion.30
  11.1 2.3 fusion.70
  13.4 1.9 collective-permute-start
  15.4 7.6 %collective-permute-start.1 = (bf16[1,256,512]{2,0,1:T(2,128)(2,1)}, bf16[1,256,512]{2,0,1:T(2,128)(2,1)}, u32[]{:S(2)}, u32[]{:S(2)}) collective-permute-start(bf16[1,256,512]{2,0,1:T(2,128)(2,1)} %get-tuple-element.150), channel_id=1, source_target_pairs={{8,0},{16,8},{24,16},{32,24},{40,32},{48,40},{56,48},{64,56},{72,6... | collective-permute-start | bytes 786440 | tf_op jit(solution)/shard_map/ppermute | solution.py:17
  23.0 2.6 collective-permute-start.2
  25.6 3.3 collective-permute-start.3
  28.8 5.6 %collective-permute-done = bf16[1,256,512]{2,0,1:T(2,128)(2,1)} collective-permute-done((bf16[1,256,512]{2,0,1:T(2,128)(2,1)}, bf16[1,256,512]{2,0,1:T(2,128)(2,1)}, u32[]{:S(2)}, u32[]{:S(2)}) %collective-permute-start) | collective-permute-done | bytes 262176 | tf_op jit(solution)/shard_map/ppermute | solution.py:14
  34.5 1.2 collective-permute-done.1
  35.6 6.2 %collective-permute-done.2 = bf16[1,256,512]{2,0,1:T(2,128)(2,1)} collective-permute-done((bf16[1,256,512]{2,0,1:T(2,128)(2,1)S(1)}, bf16[1,256,512]{2,0,1:T(2,128)(2,1)}, u32[]{:S(2)}, u32[]{:S(2)}) %collective-permute-start.2) | collective-permute-done | bytes 262176 | tf_op jit(solution)/shard_map/ppermute | solution.py:14
  41.8 5.4 %collective-permute-done.3 = bf16[1,256,512]{2,0,1:T(2,128)(2,1)} collective-permute-done((bf16[1,256,512]{2,0,1:T(2,128)(2,1)S(1)}, bf16[1,256,512]{2,0,1:T(2,128)(2,1)}, u32[]{:S(2)}, u32[]{:S(2)}) %collective-permute-start.3) | collective-permute-done | bytes 262176 | tf_op jit(solution)/shard_map/ppermute | solution.py:17
  47.2 4.5 %convolution_convert_fusion.1 = bf16[4,256,512]{2,0,1:T(4,128)(2,1)S(1)} fusion(bf16[4,256,512]{2,0,1:T(4,128)(2,1)S(1)} %convolution_convert_fusion.2, bf16[1,256,512]{2,0,1:T(2,128)(2,1)} %collective-permute-done.3, bf16[1,256,512]{2,0,1:T(2,128)(2,1)} %collective-permute-done.2, bf16[1,256,512]{2,0,1:T(2,128)(2,1)} %collective-permute-done.1, ...), kind=kOutput, calls=%fused_computation.36 | convolution fusion | flops 11010064 | bytes 3145760 | tf_op jit(solution)/shard_map/ds,dnj->snj/dot_general | solution.py:63
  51.7 1.4 fusion.27
  54.5 1.7 convolution_bitcast_fusion.2
  57.9 75.5 %all-reduce.2.cloned.1.call-done = f32[1,256,128]{2,1,0:T(8,128)} async-done(((f32[1,256,128]{2,1,0:T(8,128)}), f32[1,256,128]{2,1,0:T(8,128)}) %all-reduce.2.cloned.1.call-update) | async-done | bytes 131088 | tf_op jit(solution)/shard_map/psum | solution.py:133
  133.9 14.5 %reshape_squeeze.6 = bf16[4,512,4,512]{3,2,1,0:T(4,128)(2,1)} reshape(bf16[1,1,2048,2048]{3,2,1,0:T(8,128)(2,1)} %param.18) | data formatting | bytes 16777216 | tf_op jit(solution)/shard_map/reshape;squeeze | solution.py:106
  148.4 6.5 %fusion.9 = f32[256,4,512,1]{2,0,3,1:T(8,128)S(1)} fusion(bf16[4,512,4,512]{3,2,1,0:T(4,128)(2,1)} %reshape_squeeze.6, bf16[4,256,512]{2,1,0:T(8,128)(2,1)} %copy-done.2, bf16[4,512]{1,0:T(4,128)(2,1)S(1)} %convert_element_type.89), kind=kOutput, calls=%fused_computation.11 | convolution fusion | flops 2149580800 | bytes 11538432 | tf_op jit(solution)/shard_map/gnj,gjfk->fnk/dot_general | solution.py:108
  155.0 22.1 %all-gather.4.cloned.1.call-done = bf16[256,2048]{1,0:T(8,128)(2,1)} async-done(((bf16[256,256]{1,0:T(8,128)(2,1)}), bf16[256,2048]{1,0:T(8,128)(2,1)}) %all-gather.4.cloned.1.call-update) | async-done | bytes 1048592 | tf_op jit(solution)/shard_map/all_gather | solution.py:126
  177.1 2.7 fusion.48
  179.8 54.5 %all-gather.6.cloned.1.call-done = f32[32,128,128]{2,1,0:T(8,128)} async-done(((f32[1,128,128]{2,1,0:T(8,128)}), f32[32,128,128]{2,1,0:T(8,128)}) %all-gather.6.cloned.1.call-update) | async-done | bytes 2097168 | tf_op jit(solution)/shard_map/all_gather | solution.py:24
  234.3 61.3 %all-gather.8.cloned.1.call-done = f32[32,256,128]{2,1,0:T(8,128)} async-done(((f32[1,256,128]{2,1,0:T(8,128)}), f32[32,256,128]{2,1,0:T(8,128)}) %all-gather.8.cloned.1.call-update) | async-done | bytes 4194320 | tf_op jit(solution)/shard_map/all_gather | solution.py:24
  295.6 71.3 %while.14 = (s32[]{:T(128)}, f32[256,128]{0,1:T(8,128)S(1)}, s32[]{:T(128)}, f32[32,128,128]{2,1,0:T(8,128)}, f32[32,256,128]{2,1,0:T(8,128)}, /*index=5*/s32[]{:T(128)}, s32[]{:T(128)}) while((s32[]{:T(128)}, f32[256,128]{0,1:T(8,128)S(1)}, s32[]{:T(128)}, f32[32,128,128]{2,1,0:T(8,128)}, f32[32,256,128]{2,1,0:T(8,128)}, ...), condition=%wide.region_3.4_spmd.clone, body=%wide.region_2.3_spmd.clone.sunk | while | flops 50462724 | bytes 1378403 | solution.py:36
  296.7 1.2 fusion.85
  298.9 1.2 fusion.85
  301.1 1.2 fusion.85
  303.3 1.2 fusion.85
  305.6 1.2 fusion.85
  307.8 1.2 fusion.85
  310.0 1.2 fusion.85
  312.2 1.2 fusion.85
  314.5 1.2 fusion.85
  316.7 1.2 fusion.85
  318.9 1.2 fusion.85
  321.2 1.2 fusion.85
  323.4 1.2 fusion.85
  325.6 1.2 fusion.85
  327.8 1.2 fusion.85
  330.1 1.2 fusion.85
  332.3 1.2 fusion.85
  334.5 1.2 fusion.85
  336.7 1.2 fusion.85
  339.0 1.2 fusion.85
  341.2 1.2 fusion.85
  343.4 1.2 fusion.85
  345.7 1.2 fusion.85
  347.9 1.2 fusion.85
  350.1 1.2 fusion.85
  352.3 1.2 fusion.85
  354.6 1.2 fusion.85
  356.8 1.2 fusion.85
  361.2 1.2 fusion.85
  365.7 1.2 fusion.85
  366.9 1.3 fusion.33
  368.7 2.8 fusion.12
  371.5 3.3 multiply_convert_fusion
  374.8 1.6 fusion.69
  376.4 2.2 collective-permute-start.4
  378.6 6.4 %collective-permute-start.5 = (bf16[1,256,512]{2,0,1:T(2,128)(2,1)S(1)}, bf16[1,256,512]{2,0,1:T(2,128)(2,1)S(1)}, u32[]{:S(2)}, u32[]{:S(2)}) collective-permute-start(bf16[1,256,512]{2,0,1:T(2,128)(2,1)S(1)} %get-tuple-element.146), channel_id=1, source_target_pairs={{8,0},{16,8},{24,16},{32,24},{40,32},{48,40},{56,48},{64,56},{72,6... | collective-permute-start | bytes 786440 | tf_op jit(solution)/shard_map/ppermute | solution.py:17
  385.0 2.1 collective-permute-start.6
  387.1 3.7 collective-permute-start.7
  390.9 5.8 %collective-permute-done.4 = bf16[1,256,512]{2,0,1:T(2,128)(2,1)S(1)} collective-permute-done((bf16[1,256,512]{2,0,1:T(2,128)(2,1)S(1)}, bf16[1,256,512]{2,0,1:T(2,128)(2,1)S(1)}, u32[]{:S(2)}, u32[]{:S(2)}) %collective-permute-start.4) | collective-permute-done | bytes 262176 | tf_op jit(solution)/shard_map/ppermute | solution.py:14
  397.1 5.4 %collective-permute-done.6 = bf16[1,256,512]{2,0,1:T(2,128)(2,1)S(1)} collective-permute-done((bf16[1,256,512]{2,0,1:T(2,128)(2,1)S(1)}, bf16[1,256,512]{2,0,1:T(2,128)(2,1)S(1)}, u32[]{:S(2)}, u32[]{:S(2)}) %collective-permute-start.6) | collective-permute-done | bytes 262176 | tf_op jit(solution)/shard_map/ppermute | solution.py:14
  402.4 5.8 %collective-permute-done.7 = bf16[1,256,512]{2,0,1:T(2,128)(2,1)S(1)} collective-permute-done((bf16[1,256,512]{2,0,1:T(2,128)(2,1)S(1)}, bf16[1,256,512]{2,0,1:T(2,128)(2,1)S(1)}, u32[]{:S(2)}, u32[]{:S(2)}) %collective-permute-start.7) | collective-permute-done | bytes 262176 | tf_op jit(solution)/shard_map/ppermute | solution.py:17
  408.2 2.9 convolution_convert_fusion
  411.1 2.2 fusion.29
  (134 shorter events, 41.5 us)
Async XLA Ops:
  6.5 46.5 %copy-start = (bf16[1,1,2048,256]{3,2,1,0:T(8,128)(2,1)S(1)}, bf16[1,1,2048,256]{3,2,1,0:T(8,128)(2,1)}, u32[]{:S(2)}) copy-start(bf16[1,1,2048,256]{3,2,1,0:T(8,128)(2,1)} %param.19) | copy-start | bytes 3145732
  6.5 126.9 %all-reduce.2.cloned.1.call-start = ((), (), s32[]{:S(2)}) async-start(), calls=%async_computation.2 | async-start | bytes 262144 | tf_op jit(solution)/shard_map/psum | solution.py:133
  6.5 3.5 copy-start.4
  11.1 36.1 %copy-start.7 = (f32[1,1,4]{2,1,0:T(1,128)S(1)}, f32[1,1,4]{2,1,0:T(1,128)}, u32[]{:S(2)}) copy-start(f32[1,1,4]{2,1,0:T(1,128)} %param.16) | copy-start | bytes 52
  13.4 21.0 %collective-permute-start = (bf16[1,256,512]{2,0,1:T(2,128)(2,1)}, bf16[1,256,512]{2,0,1:T(2,128)(2,1)}, u32[]{:S(2)}, u32[]{:S(2)}) collective-permute-start(bf16[1,256,512]{2,0,1:T(2,128)(2,1)} %get-tuple-element.147), channel_id=1, source_target_pairs={{0,8},{8,16},{16,24},{24,32},{32,40},{40,48},{48,56},{56,64},{64,7... | collective-permute-start | bytes 786440 | tf_op jit(solution)/shard_map/ppermute | solution.py:14
  15.4 20.3 %collective-permute-start.1 = (bf16[1,256,512]{2,0,1:T(2,128)(2,1)}, bf16[1,256,512]{2,0,1:T(2,128)(2,1)}, u32[]{:S(2)}, u32[]{:S(2)}) collective-permute-start(bf16[1,256,512]{2,0,1:T(2,128)(2,1)} %get-tuple-element.150), channel_id=1, source_target_pairs={{8,0},{16,8},{24,16},{32,24},{40,32},{48,40},{56,48},{64,56},{72,6... | collective-permute-start | bytes 786440 | tf_op jit(solution)/shard_map/ppermute | solution.py:17
  23.0 18.8 %collective-permute-start.2 = (bf16[1,256,512]{2,0,1:T(2,128)(2,1)S(1)}, bf16[1,256,512]{2,0,1:T(2,128)(2,1)}, u32[]{:S(2)}, u32[]{:S(2)}) collective-permute-start(bf16[1,256,512]{2,0,1:T(2,128)(2,1)S(1)} %get-tuple-element.149), channel_id=1, source_target_pairs={{0,1},{1,2},{2,3},{3,4},{4,5},{5,6},{6,7},{8,9},{9,10},{10,11},{11... | collective-permute-start | bytes 786440 | tf_op jit(solution)/shard_map/ppermute | solution.py:14
  25.6 21.6 %collective-permute-start.3 = (bf16[1,256,512]{2,0,1:T(2,128)(2,1)S(1)}, bf16[1,256,512]{2,0,1:T(2,128)(2,1)}, u32[]{:S(2)}, u32[]{:S(2)}) collective-permute-start(bf16[1,256,512]{2,0,1:T(2,128)(2,1)S(1)} %get-tuple-element.148), channel_id=1, source_target_pairs={{1,0},{2,1},{3,2},{4,3},{5,4},{6,5},{7,6},{9,8},{10,9},{11,10},{12... | collective-permute-start | bytes 786440 | tf_op jit(solution)/shard_map/ppermute | solution.py:17
  47.2 4.5 %copy-start.3 = (s32[1,1,4,512]{3,2,1,0:T(4,128)S(1)}, s32[1,1,4,512]{3,2,1,0:T(4,128)}, u32[]{:S(2)}) copy-start(s32[1,1,4,512]{3,2,1,0:T(4,128)} %param.15) | copy-start | bytes 24580
  53.1 1.0 copy-start.2
  53.1 80.5 %copy-start.6 = (s32[1,1,256]{2,1,0:T(1,128)S(1)}, s32[1,1,256]{2,1,0:T(1,128)}, u32[]{:S(2)}) copy-start(s32[1,1,256]{2,1,0:T(1,128)} %param.17) | copy-start | bytes 3076
  54.5 1.8 copy-start.1
  56.2 120.8 %all-gather.4.cloned.1.call-start = ((), (), s32[]{:S(2)}) async-start(), calls=%async_computation | async-start | bytes 1179648 | tf_op jit(solution)/shard_map/all_gather | solution.py:126
  57.0 177.3 %all-gather.6.cloned.1.call-start = ((), (), s32[]{:S(2)}) async-start(), calls=%async_computation.1 | async-start | bytes 2162688 | tf_op jit(solution)/shard_map/all_gather | solution.py:24
  57.7 237.9 %all-gather.8.cloned.1.call-start = ((), (), s32[]{:S(2)}) async-start(), calls=%async_computation.3 | async-start | bytes 4325376 | tf_op jit(solution)/shard_map/all_gather | solution.py:24
  368.7 2.8 copy-start.5
  368.7 2.8 copy-start.8
  376.4 20.3 %collective-permute-start.4 = (bf16[1,256,512]{2,0,1:T(2,128)(2,1)S(1)}, bf16[1,256,512]{2,0,1:T(2,128)(2,1)S(1)}, u32[]{:S(2)}, u32[]{:S(2)}) collective-permute-start(bf16[1,256,512]{2,0,1:T(2,128)(2,1)S(1)} %get-tuple-element.143), channel_id=1, source_target_pairs={{0,8},{8,16},{16,24},{24,32},{32,40},{40,48},{48,56},{56,64},{64,7... | collective-permute-start | bytes 786440 | tf_op jit(solution)/shard_map/ppermute | solution.py:14
  378.6 18.5 %collective-permute-start.5 = (bf16[1,256,512]{2,0,1:T(2,128)(2,1)S(1)}, bf16[1,256,512]{2,0,1:T(2,128)(2,1)S(1)}, u32[]{:S(2)}, u32[]{:S(2)}) collective-permute-start(bf16[1,256,512]{2,0,1:T(2,128)(2,1)S(1)} %get-tuple-element.146), channel_id=1, source_target_pairs={{8,0},{16,8},{24,16},{32,24},{40,32},{48,40},{56,48},{64,56},{72,6... | collective-permute-start | bytes 786440 | tf_op jit(solution)/shard_map/ppermute | solution.py:17
  385.0 17.5 %collective-permute-start.6 = (bf16[1,256,512]{2,0,1:T(2,128)(2,1)S(1)}, bf16[1,256,512]{2,0,1:T(2,128)(2,1)S(1)}, u32[]{:S(2)}, u32[]{:S(2)}) collective-permute-start(bf16[1,256,512]{2,0,1:T(2,128)(2,1)S(1)} %get-tuple-element.145), channel_id=1, source_target_pairs={{0,1},{1,2},{2,3},{3,4},{4,5},{5,6},{6,7},{8,9},{9,10},{10,11},{11... | collective-permute-start | bytes 786440 | tf_op jit(solution)/shard_map/ppermute | solution.py:14
  387.1 21.1 %collective-permute-start.7 = (bf16[1,256,512]{2,0,1:T(2,128)(2,1)S(1)}, bf16[1,256,512]{2,0,1:T(2,128)(2,1)S(1)}, u32[]{:S(2)}, u32[]{:S(2)}) collective-permute-start(bf16[1,256,512]{2,0,1:T(2,128)(2,1)S(1)} %get-tuple-element.144), channel_id=1, source_target_pairs={{1,0},{2,1},{3,2},{4,3},{5,4},{6,5},{7,6},{9,8},{10,9},{11,10},{12... | collective-permute-start | bytes 786440 | tf_op jit(solution)/shard_map/ppermute | solution.py:17
Sparse Core Ops, SparseCore 0:
  56.3 77.0 all-reduce.1
  135.3 41.7 all-gather.3
  180.0 54.2 all-gather.5
  237.0 58.5 all-gather.7
where the time goes:
time: 423 us; the launch traced here: 420 us
  waiting for transfers between devices  251 us (59%)
  matrix products  70.6 us (17%)
  local copies, waits for them, and re-layouts  53.2 us (13%)
  starting transfers between devices  30.1 us (7%)
  between operations  13.4 us (3%)
    all_gather x2, waiting for transfers between devices, carried_in(): everything = jax.tree.map(lambda part: lax.all_gather(part, axis), array)  116 us
    psum x1, waiting for transfers between devices, per_device(): lax.psum(jnp.dot(coarse_residual, own_rows, preferred_element_type=jnp.fl...  75.5 us
    dot_general x32, matrix products, compose(): joined_state = jnp.dot(earlier[1], later[0], precision=HIGHEST) + later[1]  37 us
    dynamic_slice x64, local copies, waits for them, and re-layouts, step(): new = combine(before, jax.tree.map(lambda part: part[k], everything))  32.4 us
    ppermute x4, waiting for transfers between devices, with_halo(): lax.ppermute(lax.slice_in_dim(block, block.shape[dim] - width, None, axis...  23 us
    all_gather x1, waiting for transfers between devices, per_device(): lax.all_gather(coarse_residual, 'coarse', axis=1, tiled=True)  22.1 us
    ppermute x4, starting transfers between devices, with_halo(): lax.ppermute(lax.slice_in_dim(block, 0, width, axis=dim), axis, backward)  21 us
    another operation x1, local copies, waits for them, and re-layouts, per_device(): front_inverse[0, 0].reshape(face_count, block_size, face_count, block_size)  14.5 us
  transfers between devices with their start and end apart: 12, of which 12 were waited for; matrix products, arithmetic and copies ran while one was open for 6% of the time, Pallas kernels for 0%

commit v1 on v0

--- a/solution.py
+++ b/solution.py
@@ -130,8 +130,11 @@
     own_rows = lax.dynamic_slice_in_dim(
         line_outflow, lax.axis_index("coarse") * primal_count, primal_count, 0
     )
-    inflow = lax.psum(
-        jnp.dot(coarse_residual, own_rows, preferred_element_type=jnp.float32), "coarse"
+    inflow = jnp.sum(
+        lax.all_gather(
+            jnp.dot(coarse_residual, own_rows, preferred_element_type=jnp.float32), "coarse"
+        ),
+        axis=0,
     )
     transfer = chain_transfer[0]
 

time: 423 us -> 385 us (0.910)
  waiting for transfers between devices: 251 us -> 210 us
    psum x1 -> x0, waiting for transfers between devices: 75.5 us -> none  [per_device(): lax.psum(jnp.dot(coarse_residual, own_rows, preferred_element_type=jnp.fl...]
    all_gather x0 -> x1, waiting for transfers between devices: none -> 38.6 us  [per_device(): lax.all_gather(jnp.dot(coarse_residual, own_rows, preferred_element_type=...]
  transfers between devices with their start and end apart: 12 -> 12, of which waited for: 12 -> 12; matrix products, arithmetic and copies ran while one was open for 6% -> 7% of each run, Pallas kernels for 0% -> 0%
where the time goes in v1:
time: 385 us; the launch traced here: 382 us
  waiting for transfers between devices  210 us (55%)
  matrix products  70.7 us (18%)
  local copies, waits for them, and re-layouts  53.2 us (14%)
  starting transfers between devices  30.1 us (8%)
  between operations  13.4 us (3%)
    all_gather x2, waiting for transfers between devices, carried_in(): everything = jax.tree.map(lambda part: lax.all_gather(part, axis), array)  115 us
    all_gather x1, waiting for transfers between devices, per_device(): lax.all_gather(jnp.dot(coarse_residual, own_rows, preferred_element_type=...  38.6 us
    dot_general x32, matrix products, compose(): joined_state = jnp.dot(earlier[1], later[0], precision=HIGHEST) + later[1]  37 us
    dynamic_slice x64, local copies, waits for them, and re-layouts, step(): new = combine(before, jax.tree.map(lambda part: part[k], everything))  32.4 us
    ppermute x4, waiting for transfers between devices, with_halo(): lax.ppermute(lax.slice_in_dim(block, block.shape[dim] - width, None, axis...  23 us
    ppermute x4, starting transfers between devices, with_halo(): lax.ppermute(lax.slice_in_dim(block, 0, width, axis=dim), axis, backward)  21 us
    all_gather x1, waiting for transfers between devices, per_device(): lax.all_gather(coarse_residual, 'coarse', axis=1, tiled=True)  19.6 us
    another operation x1, local copies, waits for them, and re-layouts, per_device(): front_inverse[0, 0].reshape(face_count, block_size, face_count, block_size)  14.5 us
  transfers between devices with their start and end apart: 12, of which 12 were waited for; matrix products, arithmetic and copies ran while one was open for 7% of the time, Pallas kernels for 0%

profile of v1, /device:TPU:26, one launch (start us, length us, event | category | flops | bytes accessed | tf_op | source)
XLA Modules:
  0.0 381.7 jit_solution(1335559288873125457)
XLA Ops:
  6.5 2.4 fusion.30
  11.1 2.3 fusion.71
  13.4 1.9 collective-permute-start
  15.4 7.6 %collective-permute-start.1 = (bf16[1,256,512]{2,0,1:T(2,128)(2,1)}, bf16[1,256,512]{2,0,1:T(2,128)(2,1)}, u32[]{:S(2)}, u32[]{:S(2)}) collective-permute-start(bf16[1,256,512]{2,0,1:T(2,128)(2,1)} %get-tuple-element.150), channel_id=1, source_target_pairs={{8,0},{16,8},{24,16},{32,24},{40,32},{48,40},{56,48},{64,56},{72,6... | collective-permute-start | bytes 786440 | tf_op jit(solution)/shard_map/ppermute | solution.py:17
  23.0 2.6 collective-permute-start.2
  25.6 3.3 collective-permute-start.3
  28.8 5.6 %collective-permute-done = bf16[1,256,512]{2,0,1:T(2,128)(2,1)} collective-permute-done((bf16[1,256,512]{2,0,1:T(2,128)(2,1)}, bf16[1,256,512]{2,0,1:T(2,128)(2,1)}, u32[]{:S(2)}, u32[]{:S(2)}) %collective-permute-start) | collective-permute-done | bytes 262176 | tf_op jit(solution)/shard_map/ppermute | solution.py:14
  34.5 1.2 collective-permute-done.1
  35.6 6.2 %collective-permute-done.2 = bf16[1,256,512]{2,0,1:T(2,128)(2,1)} collective-permute-done((bf16[1,256,512]{2,0,1:T(2,128)(2,1)S(1)}, bf16[1,256,512]{2,0,1:T(2,128)(2,1)}, u32[]{:S(2)}, u32[]{:S(2)}) %collective-permute-start.2) | collective-permute-done | bytes 262176 | tf_op jit(solution)/shard_map/ppermute | solution.py:14
  41.8 5.4 %collective-permute-done.3 = bf16[1,256,512]{2,0,1:T(2,128)(2,1)} collective-permute-done((bf16[1,256,512]{2,0,1:T(2,128)(2,1)S(1)}, bf16[1,256,512]{2,0,1:T(2,128)(2,1)}, u32[]{:S(2)}, u32[]{:S(2)}) %collective-permute-start.3) | collective-permute-done | bytes 262176 | tf_op jit(solution)/shard_map/ppermute | solution.py:17
  47.2 4.5 %convolution_convert_fusion.1 = bf16[4,256,512]{2,0,1:T(4,128)(2,1)S(1)} fusion(bf16[4,256,512]{2,0,1:T(4,128)(2,1)S(1)} %convolution_convert_fusion.2, bf16[1,256,512]{2,0,1:T(2,128)(2,1)} %collective-permute-done.3, bf16[1,256,512]{2,0,1:T(2,128)(2,1)} %collective-permute-done.2, bf16[1,256,512]{2,0,1:T(2,128)(2,1)} %collective-permute-done.1, ...), kind=kOutput, calls=%fused_computation.36 | convolution fusion | flops 11010064 | bytes 3145760 | tf_op jit(solution)/shard_map/ds,dnj->snj/dot_general | solution.py:63
  51.7 1.4 fusion.27
  54.5 1.7 fusion.59
  57.9 38.6 %all-gather.11.cloned.1.call-done = f32[2048,128]{1,0:T(8,128)} async-done(((f32[256,128]{1,0:T(8,128)}), f32[2048,128]{1,0:T(8,128)}) %all-gather.11.cloned.1.call-update) | async-done | bytes 1048592 | tf_op jit(solution)/shard_map/all_gather | solution.py:134
  96.5 1.9 reduce_sum.19
  98.8 14.5 %reshape_squeeze.6 = bf16[4,512,4,512]{3,2,1,0:T(4,128)(2,1)} reshape(bf16[1,1,2048,2048]{3,2,1,0:T(8,128)(2,1)} %param.18) | data formatting | bytes 16777216 | tf_op jit(solution)/shard_map/reshape;squeeze | solution.py:106
  113.4 6.6 %fusion.9 = f32[256,4,512,1]{2,0,3,1:T(8,128)S(1)} fusion(bf16[4,512,4,512]{3,2,1,0:T(4,128)(2,1)} %reshape_squeeze.6, bf16[4,256,512]{2,1,0:T(8,128)(2,1)} %copy-done.2, bf16[4,512]{1,0:T(4,128)(2,1)S(1)} %convert_element_type.89), kind=kOutput, calls=%fused_computation.11 | convolution fusion | flops 2149580800 | bytes 11538432 | tf_op jit(solution)/shard_map/gnj,gjfk->fnk/dot_general | solution.py:108
  120.0 19.6 %all-gather.7.cloned.1.call-done = bf16[256,2048]{1,0:T(8,128)(2,1)} async-done(((bf16[256,256]{1,0:T(8,128)(2,1)}), bf16[256,2048]{1,0:T(8,128)(2,1)}) %all-gather.7.cloned.1.call-update) | async-done | bytes 1048592 | tf_op jit(solution)/shard_map/all_gather | solution.py:126
  139.6 2.7 fusion.48
  142.2 54.2 %all-gather.9.cloned.1.call-done = f32[32,128,128]{2,1,0:T(8,128)} async-done(((f32[1,128,128]{2,1,0:T(8,128)}), f32[32,128,128]{2,1,0:T(8,128)}) %all-gather.9.cloned.1.call-update) | async-done | bytes 2097168 | tf_op jit(solution)/shard_map/all_gather | solution.py:24
  196.5 61.0 %all-gather.13.cloned.1.call-done = f32[8192,128]{1,0:T(8,128)} async-done(((f32[256,128]{1,0:T(8,128)}), f32[8192,128]{1,0:T(8,128)}) %all-gather.13.cloned.1.call-update) | async-done | bytes 4194320 | tf_op jit(solution)/shard_map/all_gather | solution.py:24
  257.4 71.3 %while.14 = (s32[]{:T(128)}, f32[256,128]{0,1:T(8,128)S(1)}, s32[]{:T(128)}, f32[32,128,128]{2,1,0:T(8,128)}, f32[32,256,128]{2,1,0:T(8,128)}, /*index=5*/s32[]{:T(128)}, s32[]{:T(128)}) while((s32[]{:T(128)}, f32[256,128]{0,1:T(8,128)S(1)}, s32[]{:T(128)}, f32[32,128,128]{2,1,0:T(8,128)}, f32[32,256,128]{2,1,0:T(8,128)}, ...), condition=%wide.region_3.4_spmd.clone, body=%wide.region_2.3_spmd.clone.sunk | while | flops 50462724 | bytes 1378403 | solution.py:36
  258.5 1.2 fusion.86
  260.7 1.2 fusion.86
  262.9 1.2 fusion.86
  265.2 1.2 fusion.86
  267.4 1.2 fusion.86
  269.6 1.2 fusion.86
  271.9 1.2 fusion.86
  274.1 1.2 fusion.86
  276.3 1.2 fusion.86
  278.5 1.2 fusion.86
  280.8 1.2 fusion.86
  283.0 1.2 fusion.86
  285.2 1.2 fusion.86
  287.4 1.2 fusion.86
  289.7 1.2 fusion.86
  291.9 1.2 fusion.86
  294.1 1.2 fusion.86
  296.4 1.2 fusion.86
  298.6 1.2 fusion.86
  300.8 1.2 fusion.86
  303.0 1.2 fusion.86
  305.3 1.2 fusion.86
  307.5 1.2 fusion.86
  309.7 1.2 fusion.86
  311.9 1.2 fusion.86
  314.2 1.2 fusion.86
  318.6 1.2 fusion.86
  323.1 1.2 fusion.86
  327.5 1.2 fusion.86
  328.7 1.3 fusion.33
  330.5 2.8 fusion.12
  333.3 3.3 multiply_convert_fusion
  336.7 1.6 fusion.70
  338.2 2.2 collective-permute-start.4
  340.4 6.4 %collective-permute-start.5 = (bf16[1,256,512]{2,0,1:T(2,128)(2,1)S(1)}, bf16[1,256,512]{2,0,1:T(2,128)(2,1)S(1)}, u32[]{:S(2)}, u32[]{:S(2)}) collective-permute-start(bf16[1,256,512]{2,0,1:T(2,128)(2,1)S(1)} %get-tuple-element.146), channel_id=1, source_target_pairs={{8,0},{16,8},{24,16},{32,24},{40,32},{48,40},{56,48},{64,56},{72,6... | collective-permute-start | bytes 786440 | tf_op jit(solution)/shard_map/ppermute | solution.py:17
  346.8 2.1 collective-permute-start.6
  349.0 3.7 collective-permute-start.7
  352.7 5.8 %collective-permute-done.4 = bf16[1,256,512]{2,0,1:T(2,128)(2,1)S(1)} collective-permute-done((bf16[1,256,512]{2,0,1:T(2,128)(2,1)S(1)}, bf16[1,256,512]{2,0,1:T(2,128)(2,1)S(1)}, u32[]{:S(2)}, u32[]{:S(2)}) %collective-permute-start.4) | collective-permute-done | bytes 262176 | tf_op jit(solution)/shard_map/ppermute | solution.py:14
  358.9 5.4 %collective-permute-done.6 = bf16[1,256,512]{2,0,1:T(2,128)(2,1)S(1)} collective-permute-done((bf16[1,256,512]{2,0,1:T(2,128)(2,1)S(1)}, bf16[1,256,512]{2,0,1:T(2,128)(2,1)S(1)}, u32[]{:S(2)}, u32[]{:S(2)}) %collective-permute-start.6) | collective-permute-done | bytes 262176 | tf_op jit(solution)/shard_map/ppermute | solution.py:14
  364.3 5.8 %collective-permute-done.7 = bf16[1,256,512]{2,0,1:T(2,128)(2,1)S(1)} collective-permute-done((bf16[1,256,512]{2,0,1:T(2,128)(2,1)S(1)}, bf16[1,256,512]{2,0,1:T(2,128)(2,1)S(1)}, u32[]{:S(2)}, u32[]{:S(2)}) %collective-permute-start.7) | collective-permute-done | bytes 262176 | tf_op jit(solution)/shard_map/ppermute | solution.py:17
  370.1 2.9 convolution_convert_fusion
  373.0 2.1 fusion.29
  (135 shorter events, 42.6 us)
Async XLA Ops:
  6.5 46.5 %copy-start = (bf16[1,1,2048,256]{3,2,1,0:T(8,128)(2,1)S(1)}, bf16[1,1,2048,256]{3,2,1,0:T(8,128)(2,1)}, u32[]{:S(2)}) copy-start(bf16[1,1,2048,256]{3,2,1,0:T(8,128)(2,1)} %param.19) | copy-start | bytes 3145732
  6.5 89.9 %all-gather.11.cloned.1.call-start = ((), (), s32[]{:S(2)}) async-start(), calls=%async_computation.2 | async-start | bytes 1179648 | tf_op jit(solution)/shard_map/all_gather | solution.py:134
  6.5 3.5 copy-start.4
  11.1 36.1 %copy-start.7 = (f32[1,1,4]{2,1,0:T(1,128)S(1)}, f32[1,1,4]{2,1,0:T(1,128)}, u32[]{:S(2)}) copy-start(f32[1,1,4]{2,1,0:T(1,128)} %param.16) | copy-start | bytes 52
  13.4 21.0 %collective-permute-start = (bf16[1,256,512]{2,0,1:T(2,128)(2,1)}, bf16[1,256,512]{2,0,1:T(2,128)(2,1)}, u32[]{:S(2)}, u32[]{:S(2)}) collective-permute-start(bf16[1,256,512]{2,0,1:T(2,128)(2,1)} %get-tuple-element.147), channel_id=1, source_target_pairs={{0,8},{8,16},{16,24},{24,32},{32,40},{40,48},{48,56},{56,64},{64,7... | collective-permute-start | bytes 786440 | tf_op jit(solution)/shard_map/ppermute | solution.py:14
  15.4 20.3 %collective-permute-start.1 = (bf16[1,256,512]{2,0,1:T(2,128)(2,1)}, bf16[1,256,512]{2,0,1:T(2,128)(2,1)}, u32[]{:S(2)}, u32[]{:S(2)}) collective-permute-start(bf16[1,256,512]{2,0,1:T(2,128)(2,1)} %get-tuple-element.150), channel_id=1, source_target_pairs={{8,0},{16,8},{24,16},{32,24},{40,32},{48,40},{56,48},{64,56},{72,6... | collective-permute-start | bytes 786440 | tf_op jit(solution)/shard_map/ppermute | solution.py:17
  23.0 18.8 %collective-permute-start.2 = (bf16[1,256,512]{2,0,1:T(2,128)(2,1)S(1)}, bf16[1,256,512]{2,0,1:T(2,128)(2,1)}, u32[]{:S(2)}, u32[]{:S(2)}) collective-permute-start(bf16[1,256,512]{2,0,1:T(2,128)(2,1)S(1)} %get-tuple-element.149), channel_id=1, source_target_pairs={{0,1},{1,2},{2,3},{3,4},{4,5},{5,6},{6,7},{8,9},{9,10},{10,11},{11... | collective-permute-start | bytes 786440 | tf_op jit(solution)/shard_map/ppermute | solution.py:14
  25.6 21.6 %collective-permute-start.3 = (bf16[1,256,512]{2,0,1:T(2,128)(2,1)S(1)}, bf16[1,256,512]{2,0,1:T(2,128)(2,1)}, u32[]{:S(2)}, u32[]{:S(2)}) collective-permute-start(bf16[1,256,512]{2,0,1:T(2,128)(2,1)S(1)} %get-tuple-element.148), channel_id=1, source_target_pairs={{1,0},{2,1},{3,2},{4,3},{5,4},{6,5},{7,6},{9,8},{10,9},{11,10},{12... | collective-permute-start | bytes 786440 | tf_op jit(solution)/shard_map/ppermute | solution.py:17
  47.2 4.5 %copy-start.3 = (s32[1,1,4,512]{3,2,1,0:T(4,128)S(1)}, s32[1,1,4,512]{3,2,1,0:T(4,128)}, u32[]{:S(2)}) copy-start(s32[1,1,4,512]{3,2,1,0:T(4,128)} %param.15) | copy-start | bytes 24580
  53.1 1.0 copy-start.2
  54.0 44.4 %copy-start.6 = (s32[1,1,256]{2,1,0:T(1,128)S(1)}, s32[1,1,256]{2,1,0:T(1,128)}, u32[]{:S(2)}) copy-start(s32[1,1,256]{2,1,0:T(1,128)} %param.17) | copy-start | bytes 3076
  54.5 1.8 copy-start.1
  56.2 83.3 %all-gather.7.cloned.1.call-start = ((), (), s32[]{:S(2)}) async-start(), calls=%async_computation | async-start | bytes 1179648 | tf_op jit(solution)/shard_map/all_gather | solution.py:126
  57.0 139.5 %all-gather.9.cloned.1.call-start = ((), (), s32[]{:S(2)}) async-start(), calls=%async_computation.1 | async-start | bytes 2162688 | tf_op jit(solution)/shard_map/all_gather | solution.py:24
  57.7 199.7 %all-gather.13.cloned.1.call-start = ((), (), s32[]{:S(2)}) async-start(), calls=%async_computation.3 | async-start | bytes 4325376 | tf_op jit(solution)/shard_map/all_gather | solution.py:24
  330.5 2.8 copy-start.5
  330.5 2.8 copy-start.8
  338.2 20.3 %collective-permute-start.4 = (bf16[1,256,512]{2,0,1:T(2,128)(2,1)S(1)}, bf16[1,256,512]{2,0,1:T(2,128)(2,1)S(1)}, u32[]{:S(2)}, u32[]{:S(2)}) collective-permute-start(bf16[1,256,512]{2,0,1:T(2,128)(2,1)S(1)} %get-tuple-element.143), channel_id=1, source_target_pairs={{0,8},{8,16},{16,24},{24,32},{32,40},{40,48},{48,56},{56,64},{64,7... | collective-permute-start | bytes 786440 | tf_op jit(solution)/shard_map/ppermute | solution.py:14
  340.4 18.5 %collective-permute-start.5 = (bf16[1,256,512]{2,0,1:T(2,128)(2,1)S(1)}, bf16[1,256,512]{2,0,1:T(2,128)(2,1)S(1)}, u32[]{:S(2)}, u32[]{:S(2)}) collective-permute-start(bf16[1,256,512]{2,0,1:T(2,128)(2,1)S(1)} %get-tuple-element.146), channel_id=1, source_target_pairs={{8,0},{16,8},{24,16},{32,24},{40,32},{48,40},{56,48},{64,56},{72,6... | collective-permute-start | bytes 786440 | tf_op jit(solution)/shard_map/ppermute | solution.py:17
  346.8 17.5 %collective-permute-start.6 = (bf16[1,256,512]{2,0,1:T(2,128)(2,1)S(1)}, bf16[1,256,512]{2,0,1:T(2,128)(2,1)S(1)}, u32[]{:S(2)}, u32[]{:S(2)}) collective-permute-start(bf16[1,256,512]{2,0,1:T(2,128)(2,1)S(1)} %get-tuple-element.145), channel_id=1, source_target_pairs={{0,1},{1,2},{2,3},{3,4},{4,5},{5,6},{6,7},{8,9},{9,10},{10,11},{11... | collective-permute-start | bytes 786440 | tf_op jit(solution)/shard_map/ppermute | solution.py:14
  349.0 21.1 %collective-permute-start.7 = (bf16[1,256,512]{2,0,1:T(2,128)(2,1)S(1)}, bf16[1,256,512]{2,0,1:T(2,128)(2,1)S(1)}, u32[]{:S(2)}, u32[]{:S(2)}) collective-permute-start(bf16[1,256,512]{2,0,1:T(2,128)(2,1)S(1)} %get-tuple-element.144), channel_id=1, source_target_pairs={{1,0},{2,1},{3,2},{4,3},{5,4},{6,5},{7,6},{9,8},{10,9},{11,10},{12... | collective-permute-start | bytes 786440 | tf_op jit(solution)/shard_map/ppermute | solution.py:17
Sparse Core Ops, SparseCore 0:
  56.3 40.1 all-gather.10
  98.2 41.3 all-gather.6
  142.1 54.2 all-gather.8
  198.9 58.5 all-gather.12
